TPU v7x, 512 devices: a whole 4x8x8 slice. The times are simulated.
512 devices in a mesh: pair: 16 (over x, y_hi, core), virt: 32 (over z, y_lo).
Axes of the slice: x: 4, y: 8 (y_hi: 2, y_lo: 4; y = y_hi * 4 + y_lo), z: 8, core: 2. Of those that a mesh axis runs over, the one named last changes fastest.
Arguments:
- amplitudes: bfloat16 [16384, 1024], P(('pair', 'virt')), may hold values from -6 to 6
- integrals: bfloat16 [1024, 65536], P('pair', 'virt'), may hold values from -0.1875 to 0.1875
- amp_mask: int32 [256, 16], P('pair'), may hold values from 0 to 1, as said below
- integral_mask: int32 [16, 1024], P('pair', 'virt'), may hold values 0 or 1
Outputs:
- ladder: bfloat16 [16384, 65536], P('pair', 'virt')
Inputs may be any that keep to these rules, and one draw needn't show every extreme that they name: `amp_mask`: 0 or 1. For every block of 16 consecutive ij tiles, the cd tiles that hold nonzeros lie within one cyclic window of cd tiles common to the block, whose length may differ from block to block.
All inputs are finite; a program needn't handle non-finite values. No bound on the sum of `integral_mask` on one device may be relied on, other than what follows from the above.
Results may differ from a plain program's by a relative error of at most 0.001.
Values may be sent and summed in bfloat16 or wider, within the bound.
No kernel may reach another device: no remote copies, remote signals or barrier semaphores. Data moves between devices by JAX's collectives and lax.ppermute only.
A program may use at most 64 MiB of HBM per device.

v0:
```python
import jax
import jax.numpy as jnp
from jax import lax
from jax.sharding import PartitionSpec as P

TILE = 64


def widened_mask(values, mask):
    tile_rows, tile_columns = mask.shape
    shaped = values.reshape(tile_rows, TILE, tile_columns, TILE)
    return (shaped * mask.astype(values.dtype)[:, None, :, None]).reshape(values.shape)


def on_device(amplitudes, integrals, amp_mask, integral_mask):
    full_amp = lax.all_gather(amplitudes, "virt", axis=0, tiled=True)
    masked_amp = widened_mask(full_amp, amp_mask)
    own_panel = widened_mask(integrals, integral_mask)
    whole_panel = lax.all_gather(own_panel, "pair", axis=0, tiled=True)
    result = jnp.dot(masked_amp, whole_panel, preferred_element_type=jnp.float32)
    return result.astype(jnp.bfloat16)


def solution(mesh):
    in_specs = (P(("pair", "virt"), None), P("pair", "virt"), P("pair", None), P("pair", "virt"))
    out_specs = P("pair", "virt")
    return jax.shard_map(
        on_device, mesh=mesh, in_specs=in_specs, out_specs=out_specs, check_vma=False
    )
```

profile of v0, /device:TPU:1, one launch (start us, length us, event | category | flops | bytes accessed | tf_op | source)
XLA Modules:
  0.0 274.7 jit_solution(16566469928729654126)
XLA Ops:
  6.5 0.0 all-gather.3.cloned.1.call-start
  6.5 0.7 all-gather.3.cloned.1.call-update
  7.3 0.0 all-gather.5.cloned.1.call-start
  7.3 0.7 convert_bitcast_fusion
  8.0 0.1 mul.32
  8.0 0.1 mul.33
  8.1 1.7 broadcast_multiply_fusion
  9.8 0.0 all-gather.5.cloned.1.call-update
  9.8 0.7 convert_element_type.9
  10.5 2.6 mul.28
  13.1 5.5 %mul.29 = bf16[1024,1024]{1,0:T(8,128)(2,1)S(1)} reshape(bf16[16,64,16,64]{3,2,1,0:T(8,128)(2,1)} %mul.28) | data formatting | bytes 4194304 | tf_op jit(solution)/shard_map/mul | solution.py:12
  18.6 134.1 %all-gather.3.cloned.1.call-done = bf16[1024,1024]{1,0:T(8,128)(2,1)} async-done(((bf16[32,1024]{1,0:T(8,128)(2,1)}), bf16[1024,1024]{1,0:T(8,128)(2,1)}) %all-gather.3.cloned.1.call-update) | async-done | bytes 2097168 | tf_op jit(solution)/shard_map/all_gather | solution.py:16
  152.8 105.7 %all-gather.5.cloned.1.call-done = bf16[1024,2048]{1,0:T(8,128)(2,1)} async-done(((bf16[64,2048]{1,0:T(8,128)(2,1)}), bf16[1024,2048]{1,0:T(8,128)(2,1)}) %all-gather.5.cloned.1.call-update) | async-done | bytes 4194320 | tf_op jit(solution)/shard_map/all_gather | solution.py:19
  258.5 9.3 %convolution_convert_fusion = bf16[1024,2048]{1,0:T(8,128)(2,1)} fusion(bf16[1024,2048]{1,0:T(8,128)(2,1)} %all-gather.5.cloned.1.call-done, bf16[1024,1024]{1,0:T(8,128)(2,1)} %all-gather.3.cloned.1.call-done, bf16[1024,1024]{1,0:T(8,128)(2,1)S(1)} %mul.29), kind=kOutput, calls=%fused_computation | convolution fusion | flops 4298113024 | bytes 12582912 | tf_op jit(solution)/shard_map/dot_general | solution.py:20
Async XLA Ops:
  6.5 146.2 %all-gather.3.cloned.1.call-start = ((), (), s32[]{:S(2)}) async-start(), calls=%async_computation | async-start | bytes 2162688 | tf_op jit(solution)/shard_map/all_gather | solution.py:16
  7.3 251.2 %all-gather.5.cloned.1.call-start = ((), (), s32[]{:S(2)}) async-start(), calls=%async_computation.1 | async-start | bytes 4456448 | tf_op jit(solution)/shard_map/all_gather | solution.py:19
Sparse Core Ops, SparseCore 0:
  9.4 143.3 all-gather.2
  156.0 102.4 all-gather.4
where the time goes:
time: 275 us
  waiting for transfers between devices  241 us (88%)
  between operations  13.4 us (5%)
  matrix products  9.34 us (3%)
  local copies, waits for them, and re-layouts  8.26 us (3%)
  other arithmetic  3.02 us (1%)
    all_gather x1, waiting for transfers between devices, on_device(): full_amp = lax.all_gather(amplitudes, 'virt', axis=0, tiled=True)  134 us
    all_gather x1, waiting for transfers between devices, on_device(): whole_panel = lax.all_gather(own_panel, 'pair', axis=0, tiled=True)  106 us
    dot_general x1, matrix products, on_device(): jnp.dot(masked_amp, whole_panel, preferred_element_type=jnp.float32)  9.34 us
    mul x4, local copies, waits for them, and re-layouts, widened_mask(): shaped * mask.astype(values.dtype)[:, None, :, None]  8.26 us
  transfers between devices with their start and end apart: 2, of which 2 were waited for; matrix products, arithmetic and copies ran while one was open for 4% of the time, Pallas kernels for 0%

commit v1 on v0

v1 whole, which is shorter than its diff:
```python
import jax
import jax.numpy as jnp
from jax import lax
from jax.experimental import pallas as pl
from jax.experimental.pallas import tpu as pltpu
from jax.sharding import Mesh, PartitionSpec as P


TILE = 64
AXES = ("x", "yh", "c", "zh", "zl", "yl")


def prep_kernel(pos, am_ref, im_ref, a_ref, b_ref, own_a_ref, own_b_ref):
    tile_row = pos[0] // 8
    lane = lax.broadcasted_iota(jnp.int32, (8, 128), 1)

    def spread(low, high):
        both = jnp.where(lane < TILE, low, high)[:1]
        return both.astype(jnp.float32).astype(jnp.bfloat16)

    for g in range(16):
        span = pl.ds(g * 128, 128)
        own_b_ref[:, span] = b_ref[:, span] * spread(im_ref[0, 2 * g], im_ref[0, 2 * g + 1])
    for g in range(8):
        span = pl.ds(g * 128, 128)
        own_a_ref[:, span] = a_ref[:, span] * spread(am_ref[tile_row, 2 * g], am_ref[tile_row, 2 * g + 1])


def prep(pos, amp_mask, integral_mask, amplitudes, integrals):
    smem, vmem = pl.BlockSpec(memory_space=pltpu.SMEM), pl.BlockSpec(memory_space=pltpu.VMEM)
    shapes = ((32, 1024), (64, 2048))
    return pl.pallas_call(
        prep_kernel,
        in_specs=[smem, smem, smem, vmem, vmem],
        out_specs=[vmem] * 2,
        out_shape=[jax.ShapeDtypeStruct(s, jnp.bfloat16) for s in shapes],
        name="prep",
    )(pos, amp_mask, integral_mask, amplitudes, integrals)


def shift_z(value, by):
    return lax.ppermute(value, ("zh", "zl"), [(z, (z + by) % 8) for z in range(8)])


def shift(value, axis, size, by):
    return lax.ppermute(value, axis, [(i, (i + by) % size) for i in range(size)])


def swap_y(value, by):
    return lax.ppermute(value, "yl", [(y, y ^ by) for y in range(4)])


def all_x(fan):
    return lax.all_to_all(fan, "x", 0, 0)


def matmul_kernel(hops, pos, *refs):
    n_in = len(hops)
    a_refs, b_refs = refs[:n_in], refs[n_in:n_in + 2]
    out_ref, a_all, b_all = refs[-3:]
    z, yl, yh, c = pos[0] // 16, lax.rem(pos[0] // 4, 4), lax.rem(pos[0] // 2, 2), lax.rem(pos[0], 2)

    @pl.when(pl.program_id(0) == 0)
    def _():
        at = 0
        for ref in a_refs:
            rows = ref.shape[0] * 128
            a_all[pl.ds(at, rows), :] = ref[...].reshape(rows, 1024)
            at += rows

    for tile in range(2):
        for side in range(2):
            inner = lax.rem(yh + tile, 2) * 2 + lax.rem(c + side, 2)
            b_all[:, inner] = b_refs[side][:, tile * TILE:(tile + 1) * TILE]
    width = out_ref.shape[-1]
    res = jnp.dot(a_all[...], b_all[...].reshape(1024, width), preferred_element_type=jnp.float32)
    res = res.astype(out_ref.dtype)
    at = 0
    for ref, hop in zip(a_refs, hops):
        for j in range(ref.shape[0]):
            step = jnp.where(c == 0, 6, 2) if hop == 2 and ref.shape[0] == 2 else hop
            block = lax.rem(z + step + 4 * j, 8)
            column = lax.rem(block, 4) if out_ref.shape[1] > 1 else 0
            for k in range(4):
                row = pl.multiple_of(jnp.bitwise_xor(yl, k) * 32, 32)
                out_ref[block // 4, column, pl.ds(row, 32), :] = res[at:at + 32]
                at += 32


def matmul(hops, pos, a_pieces, b_pieces, base=None, width=512):
    if base is None:
        out_spec = pl.BlockSpec((2, 4, 128, width), lambda s, pos: (0, 0, 0, s))
    else:
        out_spec = pl.BlockSpec((2, 1, 128, width), lambda s, pos: (0, lax.rem(pos[0] // 16 + hops[0], 4), 0, s))
    rows = sum(p.shape[0] for p in a_pieces) * 128
    grid_spec = pltpu.PrefetchScalarGridSpec(
        num_scalar_prefetch=1,
        grid=(2048 // width,),
        in_specs=[pl.BlockSpec(p.shape, lambda s, pos: (0, 0, 0)) for p in a_pieces]
        + [pl.BlockSpec((4, 128, width), lambda s, pos: (0, 0, s))] * 2
        + ([] if base is None else [pl.BlockSpec(memory_space=pl.ANY)]),
        out_specs=out_spec,
        scratch_shapes=[pltpu.VMEM((rows, 1024), jnp.bfloat16), pltpu.VMEM((4, 4, 64, width), jnp.bfloat16)],
    )
    more = () if base is None else (base,)
    return pl.pallas_call(
        lambda *refs: matmul_kernel(hops, *refs),
        grid_spec=grid_spec,
        out_shape=jax.ShapeDtypeStruct((2, 4, 128, 2048), jnp.bfloat16),
        input_output_aliases={} if base is None else {1 + len(a_pieces) + 2: 0},
        name="ladder_matmul" if base is None else "ladder_last",
    )(pos, *a_pieces, *b_pieces, *more)


def on_device(amplitudes, integrals, amp_mask, integral_mask):
    virt = (lax.axis_index("zh") * 4 + lax.axis_index("zl")) * 4 + lax.axis_index("yl")
    pos = (virt * 4 + lax.axis_index("yh") * 2 + lax.axis_index("c")).reshape(1)
    own_a, own_b = prep(pos, amp_mask, integral_mask, amplitudes, integrals)
    far_b = shift(own_b, "yh", 2, 1)
    a_two = jnp.concatenate([own_a[None, None], shift_z(own_a, 4)[None, None]])
    a0 = jnp.concatenate([a_two] + [swap_y(a_two, k) for k in (1, 2, 3)], axis=1)
    a0 = a0.reshape(2, 128, 1024)
    here = all_x(jnp.broadcast_to(jnp.concatenate([own_b, far_b])[None], (4, 128, 2048)))
    there = shift(here, "c", 2, 1)
    b_pieces = [here, there]
    a1, a3 = shift_z(a0, -1), shift_z(a0, 1)
    f1, f3 = shift_z(a1[:1], -1), shift_z(a3[:1], 1)
    out = matmul((0, 1, 7, 2, 6), pos, [a0, a1, a3, f1, f3], b_pieces)
    return out.reshape(1024, 2048)


def solution(mesh):
    fine = Mesh(mesh.devices.reshape(4, 2, 2, 2, 4, 4), AXES)
    pair, virt = AXES[:3], AXES[3:]
    in_specs = (P(AXES, None), P(pair, virt), P(pair, None), P(pair, virt))
    return jax.shard_map(on_device, mesh=fine, in_specs=in_specs, out_specs=P(pair, virt), check_vma=False)
```

time: 275 us -> 125 us (0.45)
  the two profiles are of different devices: /device:TPU:1 before, /device:TPU:32 now
where the time goes in v1:
time: 125 us; the launch traced here: 124 us
  starting transfers between devices  44.7 us (36%)
  waiting for transfers between devices  37.7 us (30%)
  blocking collectives  28.4 us (23%)
  Pallas kernels  10.4 us (8%)
  local copies, waits for them, and re-layouts  1.82 us (1%)
    all_to_all x1, blocking collectives, all_x(): return lax.all_to_all(fan, 'x', 0, 0)  28.4 us
    ppermute x5, starting transfers between devices, shift_z(): lax.ppermute(value, ('zh', 'zl'), [(z, (z + by) % 8) for z in range(8)])  24.7 us
    ppermute x5, waiting for transfers between devices, shift_z(): lax.ppermute(value, ('zh', 'zl'), [(z, (z + by) % 8) for z in range(8)])  17.9 us
    ppermute x2, waiting for transfers between devices, shift(): lax.ppermute(value, axis, [(i, (i + by) % size) for i in range(size)])  12.3 us
    ppermute x3, starting transfers between devices, swap_y(): return lax.ppermute(value, 'yl', [(y, y ^ by) for y in range(4)])  10.7 us
    ppermute x2, starting transfers between devices, shift(): lax.ppermute(value, axis, [(i, (i + by) % size) for i in range(size)])  9.26 us
    pallas_call x1, Pallas kernels, matmul(): pl.pallas_call(lambda *refs: matmul_kernel(hops, *refs), grid_spec=grid_s...  8.63 us
    ppermute x3, waiting for transfers between devices, swap_y(): return lax.ppermute(value, 'yl', [(y, y ^ by) for y in range(4)])  7.47 us
  transfers between devices with their start and end apart: 10, of which 6 were waited for; matrix products, arithmetic and copies ran while one was open for 0% of the time, Pallas kernels for 0%

profile of v1, /device:TPU:32, one launch (start us, length us, event | category | flops | bytes accessed | tf_op | source)
XLA Modules:
  0.0 124.2 jit_solution(847429718049745482)
XLA Ops:
  0.0 1.8 %prep.1 = (bf16[32,1024]{1,0:T(8,128)(2,1)}, bf16[64,2048]{1,0:T(8,128)(2,1)}) custom-call(s32[1]{0:T(128)} %bitcast.pos.refs_0_, s32[16,16]{1,0:T(8,128)} %am_ref.1, s32[1,32]{1,0:T(1,128)} %im_ref.1, bf16[32,1024]{1,0:T(8,128)(2,1)} %a_ref.1, bf16[64,2048]{1,0:T(8,128)(2,1)} %b_ref.1), custom_call_target="tpu_custom_call" | custom-call | tf_op jit(solution)/shard_map/prep/pallas_call | solution.py:32
  1.8 7.3 %collective-permute-start.8 = (bf16[64,2048]{1,0:T(8,128)(2,1)}, bf16[64,2048]{1,0:T(8,128)(2,1)S(1)}, u32[]{:S(2)}, u32[]{:S(2)}) collective-permute-start(bf16[64,2048]{1,0:T(8,128)(2,1)} %get-tuple-element.8), channel_id=1, source_target_pairs={{0,64},{64,0},{1,65},{65,1},{2,66},{66,2},{3,67},{67,3},{4,68},{68... | collective-permute-start | bytes 786440 | tf_op jit(solution)/shard_map/ppermute | solution.py:46
  9.1 12.3 %collective-permute-done.8 = bf16[64,2048]{1,0:T(8,128)(2,1)S(1)} collective-permute-done((bf16[64,2048]{1,0:T(8,128)(2,1)}, bf16[64,2048]{1,0:T(8,128)(2,1)S(1)}, u32[]{:S(2)}, u32[]{:S(2)}) %collective-permute-start.8) | collective-permute-done | bytes 262176 | tf_op jit(solution)/shard_map/ppermute | solution.py:46
  21.5 1.0 pad_maximum_fusion.1
  22.4 0.2 broadcast_in_dim.14
  22.7 0.0 copy-start.4
  22.7 28.4 %all_to_all.5.refs_6_ = bf16[4,128,2048]{2,1,0:T(8,128)(2,1)S(1)} all-to-all(bf16[4,128,2048]{2,1,0:T(8,128)(2,1)S(1)} %broadcast_in_dim.14), channel_id=1, replica_groups=mesh['x'=4,'yh'=2,'c'=2,'zh'=2,'zl'=4,'yl'=4] {'x'}, dimensions={0} | all-to-all | bytes 4194304 | tf_op jit(solution)/shard_map/all_to_all | solution.py:54
  51.1 1.9 %collective-permute-start.9 = (bf16[4,128,2048]{2,1,0:T(8,128)(2,1)S(1)}, bf16[4,128,2048]{2,1,0:T(8,128)(2,1)}, u32[]{:S(2)}, u32[]{:S(2)}) collective-permute-start(bf16[4,128,2048]{2,1,0:T(8,128)(2,1)S(1)} %all_to_all.5.refs_6_), channel_id=1, source_target_pairs={{0,32},{32,0},{1,33},{33,1},{2,34},{34,2},{3,35},{35,3},{4,36},{36... | collective-permute-start | bytes 6291464 | tf_op jit(solution)/shard_map/ppermute | solution.py:46
  53.0 0.0 copy-done.4
  53.0 8.5 %collective-permute-start = (bf16[32,1024]{1,0:T(8,128)(2,1)S(1)}, bf16[32,1024]{1,0:T(8,128)(2,1)S(1)}, u32[]{:S(2)}, u32[]{:S(2)}) collective-permute-start(bf16[32,1024]{1,0:T(8,128)(2,1)S(1)} %copy-done.4), channel_id=1, source_target_pairs={{0,16},{4,20},{8,24},{12,28},{16,0},{20,4},{24,8},{28,12},{1,17},{... | collective-permute-start | bytes 196616 | tf_op jit(solution)/shard_map/ppermute | solution.py:42
  61.5 2.8 %collective-permute-done = bf16[32,1024]{1,0:T(8,128)(2,1)S(1)} collective-permute-done((bf16[32,1024]{1,0:T(8,128)(2,1)S(1)}, bf16[32,1024]{1,0:T(8,128)(2,1)S(1)}, u32[]{:S(2)}, u32[]{:S(2)}) %collective-permute-start) | collective-permute-done | bytes 65568 | tf_op jit(solution)/shard_map/ppermute | solution.py:42
  64.3 6.3 %collective-permute-start.3 = (bf16[2,1,32,1024]{3,2,1,0:T(8,128)(2,1)S(1)}, bf16[2,1,32,1024]{3,2,1,0:T(8,128)(2,1)S(1)}, u32[]{:S(2)}, u32[]{:S(2)}) collective-permute-start(bf16[2,1,32,1024]{3,2,1,0:T(8,128)(2,1)S(1)} %pad_maximum_fusion.2), channel_id=1, source_target_pairs={{0,3},{1,2},{2,1},{3,0},{4,7},{5,6},{6,5},{7,4},{8,11},{9,10},{10,... | collective-permute-start | bytes 393224 | tf_op jit(solution)/shard_map/ppermute | solution.py:50
  70.6 1.9 %collective-permute-start.2 = (bf16[2,1,32,1024]{3,2,1,0:T(8,128)(2,1)S(1)}, bf16[2,1,32,1024]{3,2,1,0:T(8,128)(2,1)S(1)}, u32[]{:S(2)}, u32[]{:S(2)}) collective-permute-start(bf16[2,1,32,1024]{3,2,1,0:T(8,128)(2,1)S(1)} %pad_maximum_fusion.2), channel_id=1, source_target_pairs={{0,2},{1,3},{2,0},{3,1},{4,6},{5,7},{6,4},{7,5},{8,10},{9,11},{10,... | collective-permute-start | bytes 393224 | tf_op jit(solution)/shard_map/ppermute | solution.py:50
  72.6 2.5 %collective-permute-start.1 = (bf16[2,1,32,1024]{3,2,1,0:T(8,128)(2,1)S(1)}, bf16[2,1,32,1024]{3,2,1,0:T(8,128)(2,1)S(1)}, u32[]{:S(2)}, u32[]{:S(2)}) collective-permute-start(bf16[2,1,32,1024]{3,2,1,0:T(8,128)(2,1)S(1)} %pad_maximum_fusion.2), channel_id=1, source_target_pairs={{0,1},{1,0},{2,3},{3,2},{4,5},{5,4},{6,7},{7,6},{8,9},{9,8},{10,11... | collective-permute-start | bytes 393224 | tf_op jit(solution)/shard_map/ppermute | solution.py:50
  75.1 0.0 collective-permute-done.3
  75.1 7.5 %collective-permute-done.2 = bf16[2,1,32,1024]{3,2,1,0:T(8,128)(2,1)S(1)} collective-permute-done((bf16[2,1,32,1024]{3,2,1,0:T(8,128)(2,1)S(1)}, bf16[2,1,32,1024]{3,2,1,0:T(8,128)(2,1)S(1)}, u32[]{:S(2)}, u32[]{:S(2)}) %collective-permute-start.2) | collective-permute-done | bytes 131104 | tf_op jit(solution)/shard_map/ppermute | solution.py:50
  82.5 0.0 collective-permute-done.1
  82.5 0.1 pad_maximum_fusion
  82.6 0.0 copy-start.1
  82.6 3.4 %collective-permute-start.5 = (bf16[2,128,1024]{2,1,0:T(8,128)(2,1)S(1)}, bf16[2,128,1024]{2,1,0:T(8,128)(2,1)S(1)}, u32[]{:S(2)}, u32[]{:S(2)}) collective-permute-start(bf16[2,128,1024]{2,1,0:T(8,128)(2,1)S(1)} %bitcast.5), channel_id=1, source_target_pairs={{0,4},{4,8},{8,12},{12,16},{16,20},{20,24},{24,28},{28,0},{1,5},{5... | collective-permute-start | bytes 1572872 | tf_op jit(solution)/shard_map/ppermute | solution.py:42
  86.0 5.8 %collective-permute-start.4 = (bf16[2,128,1024]{2,1,0:T(8,128)(2,1)S(1)}, bf16[2,128,1024]{2,1,0:T(8,128)(2,1)S(1)}, u32[]{:S(2)}, u32[]{:S(2)}) collective-permute-start(bf16[2,128,1024]{2,1,0:T(8,128)(2,1)S(1)} %bitcast.6), channel_id=1, source_target_pairs={{0,28},{4,0},{8,4},{12,8},{16,12},{20,16},{24,20},{28,24},{1,29},{... | collective-permute-start | bytes 1572872 | tf_op jit(solution)/shard_map/ppermute | solution.py:42
  91.9 10.2 %collective-permute-done.5.refs_3_ = bf16[2,128,1024]{2,1,0:T(8,128)(2,1)S(1)} collective-permute-done((bf16[2,128,1024]{2,1,0:T(8,128)(2,1)S(1)}, bf16[2,128,1024]{2,1,0:T(8,128)(2,1)S(1)}, u32[]{:S(2)}, u32[]{:S(2)}) %collective-permute-start.5) | collective-permute-done | bytes 524320 | tf_op jit(solution)/shard_map/ppermute | solution.py:42
  102.0 1.9 %collective-permute-start.7 = (bf16[1,128,1024]{2,1,0:T(8,128)(2,1)S(1)}, bf16[1,128,1024]{2,1,0:T(8,128)(2,1)S(1)}, u32[]{:S(2)}, u32[]{:S(2)}) collective-permute-start(bf16[1,128,1024]{2,1,0:T(8,128)(2,1)S(1)} %slice.9), channel_id=1, source_target_pairs={{0,4},{4,8},{8,12},{12,16},{16,20},{20,24},{24,28},{28,0},{1,5},{5... | collective-permute-start | bytes 786440 | tf_op jit(solution)/shard_map/ppermute | solution.py:42
  104.0 0.0 collective-permute-done.4.refs_2_
  104.0 0.8 copy-done.3
  104.8 5.1 %collective-permute-start.6 = (bf16[1,128,1024]{2,1,0:T(8,128)(2,1)S(1)}, bf16[1,128,1024]{2,1,0:T(8,128)(2,1)S(1)}, u32[]{:S(2)}, u32[]{:S(2)}) collective-permute-start(bf16[1,128,1024]{2,1,0:T(8,128)(2,1)S(1)} %slice.8), channel_id=1, source_target_pairs={{0,28},{4,0},{8,4},{12,8},{16,12},{20,16},{24,20},{28,24},{1,29},{... | collective-permute-start | bytes 786440 | tf_op jit(solution)/shard_map/ppermute | solution.py:42
  110.0 2.8 %collective-permute-done.7.refs_5_ = bf16[1,128,1024]{2,1,0:T(8,128)(2,1)S(1)} collective-permute-done((bf16[1,128,1024]{2,1,0:T(8,128)(2,1)S(1)}, bf16[1,128,1024]{2,1,0:T(8,128)(2,1)S(1)}, u32[]{:S(2)}, u32[]{:S(2)}) %collective-permute-start.7) | collective-permute-done | bytes 262176 | tf_op jit(solution)/shard_map/ppermute | solution.py:42
  112.8 2.0 %collective-permute-done.6.refs_4_ = bf16[1,128,1024]{2,1,0:T(8,128)(2,1)S(1)} collective-permute-done((bf16[1,128,1024]{2,1,0:T(8,128)(2,1)S(1)}, bf16[1,128,1024]{2,1,0:T(8,128)(2,1)S(1)}, u32[]{:S(2)}, u32[]{:S(2)}) %collective-permute-start.6) | collective-permute-done | bytes 262176 | tf_op jit(solution)/shard_map/ppermute | solution.py:42
  114.8 0.7 copy-done.6
  115.5 0.0 collective-permute-done.9.refs_7_
  115.5 0.0 copy-done.1
  115.6 8.6 %ladder_matmul.1 = bf16[2,4,128,2048]{3,2,1,0:T(8,128)(2,1)} custom-call(s32[1]{0:T(128)} %bitcast.pos.refs_0_, bf16[2,128,1024]{2,1,0:T(8,128)(2,1)} %bitcast.7, bf16[2,128,1024]{2,1,0:T(8,128)(2,1)} %copy-done.3, bf16[2,128,1024]{2,1,0:T(8,128)(2,1)} %copy-done.2, bf16[1,128,1024]{2,1,0:T(8,128)(2,1)} %copy-done.6, bf16[1,128,1024]{2,1,0:T(8,128)(2,1)} %copy-done.5, ...), custom_call_target="tpu_custom_call" | custom-call | tf_op jit(solution)/shard_map/ladder_matmul/pallas_call | solution.py:106
  (11 shorter events, 0.1 us)
Async XLA Ops:
  1.8 19.7 %collective-permute-start.8 = (bf16[64,2048]{1,0:T(8,128)(2,1)}, bf16[64,2048]{1,0:T(8,128)(2,1)S(1)}, u32[]{:S(2)}, u32[]{:S(2)}) collective-permute-start(bf16[64,2048]{1,0:T(8,128)(2,1)} %get-tuple-element.8), channel_id=1, source_target_pairs={{0,64},{64,0},{1,65},{65,1},{2,66},{66,2},{3,67},{67,3},{4,68},{68... | collective-permute-start | bytes 786440 | tf_op jit(solution)/shard_map/ppermute | solution.py:46
  22.7 30.3 %copy-start.4 = (bf16[32,1024]{1,0:T(8,128)(2,1)S(1)}, bf16[32,1024]{1,0:T(8,128)(2,1)}, u32[]{:S(2)}) copy-start(bf16[32,1024]{1,0:T(8,128)(2,1)} %get-tuple-element.7) | copy-start | bytes 196612
  51.1 64.5 %copy-start = (bf16[4,128,2048]{2,1,0:T(8,128)(2,1)}, bf16[4,128,2048]{2,1,0:T(8,128)(2,1)S(1)}, u32[]{:S(2)}) copy-start(bf16[4,128,2048]{2,1,0:T(8,128)(2,1)S(1)} %all_to_all.5.refs_6_) | copy-start | bytes 6291460
  51.1 64.5 %collective-permute-start.9 = (bf16[4,128,2048]{2,1,0:T(8,128)(2,1)S(1)}, bf16[4,128,2048]{2,1,0:T(8,128)(2,1)}, u32[]{:S(2)}, u32[]{:S(2)}) collective-permute-start(bf16[4,128,2048]{2,1,0:T(8,128)(2,1)S(1)} %all_to_all.5.refs_6_), channel_id=1, source_target_pairs={{0,32},{32,0},{1,33},{33,1},{2,34},{34,2},{3,35},{35,3},{4,36},{36... | collective-permute-start | bytes 6291464 | tf_op jit(solution)/shard_map/ppermute | solution.py:46
  53.0 11.3 %collective-permute-start = (bf16[32,1024]{1,0:T(8,128)(2,1)S(1)}, bf16[32,1024]{1,0:T(8,128)(2,1)S(1)}, u32[]{:S(2)}, u32[]{:S(2)}) collective-permute-start(bf16[32,1024]{1,0:T(8,128)(2,1)S(1)} %copy-done.4), channel_id=1, source_target_pairs={{0,16},{4,20},{8,24},{12,28},{16,0},{20,4},{24,8},{28,12},{1,17},{... | collective-permute-start | bytes 196616 | tf_op jit(solution)/shard_map/ppermute | solution.py:42
  64.3 10.7 %collective-permute-start.3 = (bf16[2,1,32,1024]{3,2,1,0:T(8,128)(2,1)S(1)}, bf16[2,1,32,1024]{3,2,1,0:T(8,128)(2,1)S(1)}, u32[]{:S(2)}, u32[]{:S(2)}) collective-permute-start(bf16[2,1,32,1024]{3,2,1,0:T(8,128)(2,1)S(1)} %pad_maximum_fusion.2), channel_id=1, source_target_pairs={{0,3},{1,2},{2,1},{3,0},{4,7},{5,6},{6,5},{7,4},{8,11},{9,10},{10,... | collective-permute-start | bytes 393224 | tf_op jit(solution)/shard_map/ppermute | solution.py:50
  70.6 11.9 %collective-permute-start.2 = (bf16[2,1,32,1024]{3,2,1,0:T(8,128)(2,1)S(1)}, bf16[2,1,32,1024]{3,2,1,0:T(8,128)(2,1)S(1)}, u32[]{:S(2)}, u32[]{:S(2)}) collective-permute-start(bf16[2,1,32,1024]{3,2,1,0:T(8,128)(2,1)S(1)} %pad_maximum_fusion.2), channel_id=1, source_target_pairs={{0,2},{1,3},{2,0},{3,1},{4,6},{5,7},{6,4},{7,5},{8,10},{9,11},{10,... | collective-permute-start | bytes 393224 | tf_op jit(solution)/shard_map/ppermute | solution.py:50
  72.6 10.0 %collective-permute-start.1 = (bf16[2,1,32,1024]{3,2,1,0:T(8,128)(2,1)S(1)}, bf16[2,1,32,1024]{3,2,1,0:T(8,128)(2,1)S(1)}, u32[]{:S(2)}, u32[]{:S(2)}) collective-permute-start(bf16[2,1,32,1024]{3,2,1,0:T(8,128)(2,1)S(1)} %pad_maximum_fusion.2), channel_id=1, source_target_pairs={{0,1},{1,0},{2,3},{3,2},{4,5},{5,4},{6,7},{7,6},{8,9},{9,8},{10,11... | collective-permute-start | bytes 393224 | tf_op jit(solution)/shard_map/ppermute | solution.py:50
  82.6 32.9 %copy-start.1 = (bf16[2,4,32,1024]{3,2,1,0:T(8,128)(2,1)}, bf16[2,4,32,1024]{3,2,1,0:T(8,128)(2,1)S(1)}, u32[]{:S(2)}) copy-start(bf16[2,4,32,1024]{3,2,1,0:T(8,128)(2,1)S(1)} %pad_maximum_fusion) | copy-start | bytes 1572868
  82.6 19.4 %collective-permute-start.5 = (bf16[2,128,1024]{2,1,0:T(8,128)(2,1)S(1)}, bf16[2,128,1024]{2,1,0:T(8,128)(2,1)S(1)}, u32[]{:S(2)}, u32[]{:S(2)}) collective-permute-start(bf16[2,128,1024]{2,1,0:T(8,128)(2,1)S(1)} %bitcast.5), channel_id=1, source_target_pairs={{0,4},{4,8},{8,12},{12,16},{16,20},{20,24},{24,28},{28,0},{1,5},{5... | collective-permute-start | bytes 1572872 | tf_op jit(solution)/shard_map/ppermute | solution.py:42
  86.0 18.0 %collective-permute-start.4 = (bf16[2,128,1024]{2,1,0:T(8,128)(2,1)S(1)}, bf16[2,128,1024]{2,1,0:T(8,128)(2,1)S(1)}, u32[]{:S(2)}, u32[]{:S(2)}) collective-permute-start(bf16[2,128,1024]{2,1,0:T(8,128)(2,1)S(1)} %bitcast.6), channel_id=1, source_target_pairs={{0,28},{4,0},{8,4},{12,8},{16,12},{20,16},{24,20},{28,24},{1,29},{... | collective-permute-start | bytes 1572872 | tf_op jit(solution)/shard_map/ppermute | solution.py:42
  102.0 13.5 %copy-start.2 = (bf16[2,128,1024]{2,1,0:T(8,128)(2,1)}, bf16[2,128,1024]{2,1,0:T(8,128)(2,1)S(1)}, u32[]{:S(2)}) copy-start(bf16[2,128,1024]{2,1,0:T(8,128)(2,1)S(1)} %collective-permute-done.5.refs_3_) | copy-start | bytes 1572868
  102.0 10.8 %collective-permute-start.7 = (bf16[1,128,1024]{2,1,0:T(8,128)(2,1)S(1)}, bf16[1,128,1024]{2,1,0:T(8,128)(2,1)S(1)}, u32[]{:S(2)}, u32[]{:S(2)}) collective-permute-start(bf16[1,128,1024]{2,1,0:T(8,128)(2,1)S(1)} %slice.9), channel_id=1, source_target_pairs={{0,4},{4,8},{8,12},{12,16},{16,20},{20,24},{24,28},{28,0},{1,5},{5... | collective-permute-start | bytes 786440 | tf_op jit(solution)/shard_map/ppermute | solution.py:42
  104.0 0.8 copy-start.3
  104.8 10.0 %collective-permute-start.6 = (bf16[1,128,1024]{2,1,0:T(8,128)(2,1)S(1)}, bf16[1,128,1024]{2,1,0:T(8,128)(2,1)S(1)}, u32[]{:S(2)}, u32[]{:S(2)}) collective-permute-start(bf16[1,128,1024]{2,1,0:T(8,128)(2,1)S(1)} %slice.8), channel_id=1, source_target_pairs={{0,28},{4,0},{8,4},{12,8},{16,12},{20,16},{24,20},{28,24},{1,29},{... | collective-permute-start | bytes 786440 | tf_op jit(solution)/shard_map/ppermute | solution.py:42
  112.8 2.8 %copy-start.5 = (bf16[1,128,1024]{2,1,0:T(8,128)(2,1)}, bf16[1,128,1024]{2,1,0:T(8,128)(2,1)S(1)}, u32[]{:S(2)}) copy-start(bf16[1,128,1024]{2,1,0:T(8,128)(2,1)S(1)} %collective-permute-done.7.refs_5_) | copy-start | bytes 786436
  114.8 0.7 copy-start.6

commit v2 on v1

--- a/solution.py
+++ b/solution.py
@@ -54,62 +54,79 @@
     return lax.all_to_all(fan, "x", 0, 0)
 
 
-def matmul_kernel(hops, pos, *refs):
+def matmul_kernel(hops, width, pos, *refs):
     n_in = len(hops)
     a_refs, b_refs = refs[:n_in], refs[n_in:n_in + 2]
-    out_ref, a_all, b_all = refs[-3:]
+    out_ref, a_all, b_all, a_sems, b_sems = refs[-5:]
+    step = pl.program_id(0)
     z, yl, yh, c = pos[0] // 16, lax.rem(pos[0] // 4, 4), lax.rem(pos[0] // 2, 2), lax.rem(pos[0], 2)
 
-    @pl.when(pl.program_id(0) == 0)
+    def b_copies(block):
+        columns = pl.ds(pl.multiple_of(block * width, width), width)
+        return [
+            pltpu.make_async_copy(
+                b_refs[side].at[:, pl.ds(tile * TILE, TILE), columns],
+                b_all.at[:, lax.rem(yh + tile, 2) * 2 + lax.rem(c + side, 2), :, columns],
+                b_sems.at[block, tile * 2 + side],
+            )
+            for tile in range(2)
+            for side in range(2)
+        ]
+
+    def a_copies():
+        copies, at = [], 0
+        for n, ref in enumerate(a_refs):
+            copies.append(pltpu.make_async_copy(ref, a_all.at[pl.ds(at, ref.shape[0])], a_sems.at[n]))
+            at += ref.shape[0]
+        return copies
+
+    @pl.when(step == 0)
     def _():
-        at = 0
-        for ref in a_refs:
-            rows = ref.shape[0] * 128
-            a_all[pl.ds(at, rows), :] = ref[...].reshape(rows, 1024)
-            at += rows
+        for copy in b_copies(0) + a_copies():
+            copy.start()
+        for block in range(1, 2048 // width):
+            for copy in b_copies(block):
+                copy.start()
+        for copy in a_copies():
+            copy.wait()
 
-    for tile in range(2):
-        for side in range(2):
-            inner = lax.rem(yh + tile, 2) * 2 + lax.rem(c + side, 2)
-            b_all[:, inner] = b_refs[side][:, tile * TILE:(tile + 1) * TILE]
-    width = out_ref.shape[-1]
-    res = jnp.dot(a_all[...], b_all[...].reshape(1024, width), preferred_element_type=jnp.float32)
-    res = res.astype(out_ref.dtype)
+    for copy in b_copies(step):
+        copy.wait()
+    columns = pl.ds(pl.multiple_of(step * width, width), width)
+    a_value = a_all[...].reshape(1024, 1024)
+    b_value = b_all[:, :, :, columns].reshape(1024, width)
+    res = jnp.dot(a_value, b_value, preferred_element_type=jnp.float32).astype(out_ref.dtype)
     at = 0
     for ref, hop in zip(a_refs, hops):
         for j in range(ref.shape[0]):
-            step = jnp.where(c == 0, 6, 2) if hop == 2 and ref.shape[0] == 2 else hop
-            block = lax.rem(z + step + 4 * j, 8)
-            column = lax.rem(block, 4) if out_ref.shape[1] > 1 else 0
+            block = lax.rem(z + hop + 4 * j, 8)
             for k in range(4):
                 row = pl.multiple_of(jnp.bitwise_xor(yl, k) * 32, 32)
-                out_ref[block // 4, column, pl.ds(row, 32), :] = res[at:at + 32]
+                out_ref[block, pl.ds(row, 32), :] = res[at:at + 32]
                 at += 32
 
 
-def matmul(hops, pos, a_pieces, b_pieces, base=None, width=512):
-    if base is None:
-        out_spec = pl.BlockSpec((2, 4, 128, width), lambda s, pos: (0, 0, 0, s))
-    else:
-        out_spec = pl.BlockSpec((2, 1, 128, width), lambda s, pos: (0, lax.rem(pos[0] // 16 + hops[0], 4), 0, s))
-    rows = sum(p.shape[0] for p in a_pieces) * 128
+def matmul(hops, pos, a_pieces, b_pieces, width=512):
+    n_in = len(hops)
+    any_spec = pl.BlockSpec(memory_space=pl.ANY)
     grid_spec = pltpu.PrefetchScalarGridSpec(
         num_scalar_prefetch=1,
         grid=(2048 // width,),
-        in_specs=[pl.BlockSpec(p.shape, lambda s, pos: (0, 0, 0)) for p in a_pieces]
-        + [pl.BlockSpec((4, 128, width), lambda s, pos: (0, 0, s))] * 2
-        + ([] if base is None else [pl.BlockSpec(memory_space=pl.ANY)]),
-        out_specs=out_spec,
-        scratch_shapes=[pltpu.VMEM((rows, 1024), jnp.bfloat16), pltpu.VMEM((4, 4, 64, width), jnp.bfloat16)],
+        in_specs=[any_spec] * (n_in + 2),
+        out_specs=pl.BlockSpec((8, 128, width), lambda s, pos: (0, 0, s)),
+        scratch_shapes=[
+            pltpu.VMEM((8, 128, 1024), jnp.bfloat16),
+            pltpu.VMEM((4, 4, 64, 2048), jnp.bfloat16),
+            pltpu.SemaphoreType.DMA((n_in,)),
+            pltpu.SemaphoreType.DMA((2048 // width, 4)),
+        ],
     )
-    more = () if base is None else (base,)
     return pl.pallas_call(
-        lambda *refs: matmul_kernel(hops, *refs),
+        lambda *refs: matmul_kernel(hops, width, *refs),
         grid_spec=grid_spec,
-        out_shape=jax.ShapeDtypeStruct((2, 4, 128, 2048), jnp.bfloat16),
-        input_output_aliases={} if base is None else {1 + len(a_pieces) + 2: 0},
-        name="ladder_matmul" if base is None else "ladder_last",
-    )(pos, *a_pieces, *b_pieces, *more)
+        out_shape=jax.ShapeDtypeStruct((8, 128, 2048), jnp.bfloat16),
+        name="ladder_matmul",
+    )(pos, *a_pieces, *b_pieces)
 
 
 def on_device(amplitudes, integrals, amp_mask, integral_mask):

time: 125 us -> 124 us (level)
  no operation moved by 1% of the time
where the time goes in v2:
time: 124 us
  starting transfers between devices  44.7 us (36%)
  waiting for transfers between devices  37.7 us (30%)
  blocking collectives  28.4 us (23%)
  Pallas kernels  9.95 us (8%)
  local copies, waits for them, and re-layouts  1.82 us (1%)
    all_to_all x1, blocking collectives, all_x(): return lax.all_to_all(fan, 'x', 0, 0)  28.4 us
    ppermute x5, starting transfers between devices, shift_z(): lax.ppermute(value, ('zh', 'zl'), [(z, (z + by) % 8) for z in range(8)])  24.7 us
    ppermute x5, waiting for transfers between devices, shift_z(): lax.ppermute(value, ('zh', 'zl'), [(z, (z + by) % 8) for z in range(8)])  17.9 us
    ppermute x2, waiting for transfers between devices, shift(): lax.ppermute(value, axis, [(i, (i + by) % size) for i in range(size)])  12.3 us
    ppermute x3, starting transfers between devices, swap_y(): return lax.ppermute(value, 'yl', [(y, y ^ by) for y in range(4)])  10.7 us
    ppermute x2, starting transfers between devices, shift(): lax.ppermute(value, axis, [(i, (i + by) % size) for i in range(size)])  9.26 us
    pallas_call x1, Pallas kernels, matmul(): pl.pallas_call(lambda *refs: matmul_kernel(hops, width, *refs), grid_spec...  8.18 us
    ppermute x3, waiting for transfers between devices, swap_y(): return lax.ppermute(value, 'yl', [(y, y ^ by) for y in range(4)])  7.47 us
  transfers between devices with their start and end apart: 10, of which 6 were waited for; matrix products, arithmetic and copies ran while one was open for 0% of the time, Pallas kernels for 0%

profile of v2, /device:TPU:32, one launch (start us, length us, event | category | flops | bytes accessed | tf_op | source)
XLA Modules:
  0.0 123.8 jit_solution(11447328469445420109)
XLA Ops:
  0.0 1.8 %prep.1 = (bf16[32,1024]{1,0:T(8,128)(2,1)}, bf16[64,2048]{1,0:T(8,128)(2,1)}) custom-call(s32[1]{0:T(128)} %bitcast.pos.refs_0_, s32[16,16]{1,0:T(8,128)} %am_ref.1, s32[1,32]{1,0:T(1,128)} %im_ref.1, bf16[32,1024]{1,0:T(8,128)(2,1)} %a_ref.1, bf16[64,2048]{1,0:T(8,128)(2,1)} %b_ref.1), custom_call_target="tpu_custom_call" | custom-call | tf_op jit(solution)/shard_map/prep/pallas_call | solution.py:32
  1.8 7.3 %collective-permute-start.8 = (bf16[64,2048]{1,0:T(8,128)(2,1)}, bf16[64,2048]{1,0:T(8,128)(2,1)S(1)}, u32[]{:S(2)}, u32[]{:S(2)}) collective-permute-start(bf16[64,2048]{1,0:T(8,128)(2,1)} %get-tuple-element.8), channel_id=1, source_target_pairs={{0,64},{64,0},{1,65},{65,1},{2,66},{66,2},{3,67},{67,3},{4,68},{68... | collective-permute-start | bytes 786440 | tf_op jit(solution)/shard_map/ppermute | solution.py:46
  9.1 12.3 %collective-permute-done.8 = bf16[64,2048]{1,0:T(8,128)(2,1)S(1)} collective-permute-done((bf16[64,2048]{1,0:T(8,128)(2,1)}, bf16[64,2048]{1,0:T(8,128)(2,1)S(1)}, u32[]{:S(2)}, u32[]{:S(2)}) %collective-permute-start.8) | collective-permute-done | bytes 262176 | tf_op jit(solution)/shard_map/ppermute | solution.py:46
  21.5 1.0 pad_maximum_fusion.1
  22.4 0.2 broadcast_in_dim.14
  22.7 0.0 copy-start.4
  22.7 28.4 %all_to_all.5.refs_6_ = bf16[4,128,2048]{2,1,0:T(8,128)(2,1)S(1)} all-to-all(bf16[4,128,2048]{2,1,0:T(8,128)(2,1)S(1)} %broadcast_in_dim.14), channel_id=1, replica_groups=mesh['x'=4,'yh'=2,'c'=2,'zh'=2,'zl'=4,'yl'=4] {'x'}, dimensions={0} | all-to-all | bytes 4194304 | tf_op jit(solution)/shard_map/all_to_all | solution.py:54
  51.1 1.9 %collective-permute-start.9 = (bf16[4,128,2048]{2,1,0:T(8,128)(2,1)S(1)}, bf16[4,128,2048]{2,1,0:T(8,128)(2,1)}, u32[]{:S(2)}, u32[]{:S(2)}) collective-permute-start(bf16[4,128,2048]{2,1,0:T(8,128)(2,1)S(1)} %all_to_all.5.refs_6_), channel_id=1, source_target_pairs={{0,32},{32,0},{1,33},{33,1},{2,34},{34,2},{3,35},{35,3},{4,36},{36... | collective-permute-start | bytes 6291464 | tf_op jit(solution)/shard_map/ppermute | solution.py:46
  53.0 0.0 copy-done.4
  53.0 8.5 %collective-permute-start = (bf16[32,1024]{1,0:T(8,128)(2,1)S(1)}, bf16[32,1024]{1,0:T(8,128)(2,1)S(1)}, u32[]{:S(2)}, u32[]{:S(2)}) collective-permute-start(bf16[32,1024]{1,0:T(8,128)(2,1)S(1)} %copy-done.4), channel_id=1, source_target_pairs={{0,16},{4,20},{8,24},{12,28},{16,0},{20,4},{24,8},{28,12},{1,17},{... | collective-permute-start | bytes 196616 | tf_op jit(solution)/shard_map/ppermute | solution.py:42
  61.5 2.8 %collective-permute-done = bf16[32,1024]{1,0:T(8,128)(2,1)S(1)} collective-permute-done((bf16[32,1024]{1,0:T(8,128)(2,1)S(1)}, bf16[32,1024]{1,0:T(8,128)(2,1)S(1)}, u32[]{:S(2)}, u32[]{:S(2)}) %collective-permute-start) | collective-permute-done | bytes 65568 | tf_op jit(solution)/shard_map/ppermute | solution.py:42
  64.3 6.3 %collective-permute-start.3 = (bf16[2,1,32,1024]{3,2,1,0:T(8,128)(2,1)S(1)}, bf16[2,1,32,1024]{3,2,1,0:T(8,128)(2,1)S(1)}, u32[]{:S(2)}, u32[]{:S(2)}) collective-permute-start(bf16[2,1,32,1024]{3,2,1,0:T(8,128)(2,1)S(1)} %pad_maximum_fusion.2), channel_id=1, source_target_pairs={{0,3},{1,2},{2,1},{3,0},{4,7},{5,6},{6,5},{7,4},{8,11},{9,10},{10,... | collective-permute-start | bytes 393224 | tf_op jit(solution)/shard_map/ppermute | solution.py:50
  70.6 1.9 %collective-permute-start.2 = (bf16[2,1,32,1024]{3,2,1,0:T(8,128)(2,1)S(1)}, bf16[2,1,32,1024]{3,2,1,0:T(8,128)(2,1)S(1)}, u32[]{:S(2)}, u32[]{:S(2)}) collective-permute-start(bf16[2,1,32,1024]{3,2,1,0:T(8,128)(2,1)S(1)} %pad_maximum_fusion.2), channel_id=1, source_target_pairs={{0,2},{1,3},{2,0},{3,1},{4,6},{5,7},{6,4},{7,5},{8,10},{9,11},{10,... | collective-permute-start | bytes 393224 | tf_op jit(solution)/shard_map/ppermute | solution.py:50
  72.6 2.5 %collective-permute-start.1 = (bf16[2,1,32,1024]{3,2,1,0:T(8,128)(2,1)S(1)}, bf16[2,1,32,1024]{3,2,1,0:T(8,128)(2,1)S(1)}, u32[]{:S(2)}, u32[]{:S(2)}) collective-permute-start(bf16[2,1,32,1024]{3,2,1,0:T(8,128)(2,1)S(1)} %pad_maximum_fusion.2), channel_id=1, source_target_pairs={{0,1},{1,0},{2,3},{3,2},{4,5},{5,4},{6,7},{7,6},{8,9},{9,8},{10,11... | collective-permute-start | bytes 393224 | tf_op jit(solution)/shard_map/ppermute | solution.py:50
  75.1 0.0 collective-permute-done.3
  75.1 7.5 %collective-permute-done.2 = bf16[2,1,32,1024]{3,2,1,0:T(8,128)(2,1)S(1)} collective-permute-done((bf16[2,1,32,1024]{3,2,1,0:T(8,128)(2,1)S(1)}, bf16[2,1,32,1024]{3,2,1,0:T(8,128)(2,1)S(1)}, u32[]{:S(2)}, u32[]{:S(2)}) %collective-permute-start.2) | collective-permute-done | bytes 131104 | tf_op jit(solution)/shard_map/ppermute | solution.py:50
  82.5 0.0 collective-permute-done.1
  82.5 0.1 pad_maximum_fusion
  82.6 0.0 copy-start.1
  82.6 3.4 %collective-permute-start.5 = (bf16[2,128,1024]{2,1,0:T(8,128)(2,1)S(1)}, bf16[2,128,1024]{2,1,0:T(8,128)(2,1)S(1)}, u32[]{:S(2)}, u32[]{:S(2)}) collective-permute-start(bf16[2,128,1024]{2,1,0:T(8,128)(2,1)S(1)} %bitcast.5), channel_id=1, source_target_pairs={{0,4},{4,8},{8,12},{12,16},{16,20},{20,24},{24,28},{28,0},{1,5},{5... | collective-permute-start | bytes 1572872 | tf_op jit(solution)/shard_map/ppermute | solution.py:42
  86.0 5.8 %collective-permute-start.4 = (bf16[2,128,1024]{2,1,0:T(8,128)(2,1)S(1)}, bf16[2,128,1024]{2,1,0:T(8,128)(2,1)S(1)}, u32[]{:S(2)}, u32[]{:S(2)}) collective-permute-start(bf16[2,128,1024]{2,1,0:T(8,128)(2,1)S(1)} %bitcast.6), channel_id=1, source_target_pairs={{0,28},{4,0},{8,4},{12,8},{16,12},{20,16},{24,20},{28,24},{1,29},{... | collective-permute-start | bytes 1572872 | tf_op jit(solution)/shard_map/ppermute | solution.py:42
  91.9 10.2 %collective-permute-done.5.refs_3_ = bf16[2,128,1024]{2,1,0:T(8,128)(2,1)S(1)} collective-permute-done((bf16[2,128,1024]{2,1,0:T(8,128)(2,1)S(1)}, bf16[2,128,1024]{2,1,0:T(8,128)(2,1)S(1)}, u32[]{:S(2)}, u32[]{:S(2)}) %collective-permute-start.5) | collective-permute-done | bytes 524320 | tf_op jit(solution)/shard_map/ppermute | solution.py:42
  102.0 1.9 %collective-permute-start.7 = (bf16[1,128,1024]{2,1,0:T(8,128)(2,1)S(1)}, bf16[1,128,1024]{2,1,0:T(8,128)(2,1)S(1)}, u32[]{:S(2)}, u32[]{:S(2)}) collective-permute-start(bf16[1,128,1024]{2,1,0:T(8,128)(2,1)S(1)} %slice.9), channel_id=1, source_target_pairs={{0,4},{4,8},{8,12},{12,16},{16,20},{20,24},{24,28},{28,0},{1,5},{5... | collective-permute-start | bytes 786440 | tf_op jit(solution)/shard_map/ppermute | solution.py:42
  104.0 0.0 collective-permute-done.4.refs_2_
  104.0 0.8 copy-done.3
  104.8 5.1 %collective-permute-start.6 = (bf16[1,128,1024]{2,1,0:T(8,128)(2,1)S(1)}, bf16[1,128,1024]{2,1,0:T(8,128)(2,1)S(1)}, u32[]{:S(2)}, u32[]{:S(2)}) collective-permute-start(bf16[1,128,1024]{2,1,0:T(8,128)(2,1)S(1)} %slice.8), channel_id=1, source_target_pairs={{0,28},{4,0},{8,4},{12,8},{16,12},{20,16},{24,20},{28,24},{1,29},{... | collective-permute-start | bytes 786440 | tf_op jit(solution)/shard_map/ppermute | solution.py:42
  110.0 2.8 %collective-permute-done.7.refs_5_ = bf16[1,128,1024]{2,1,0:T(8,128)(2,1)S(1)} collective-permute-done((bf16[1,128,1024]{2,1,0:T(8,128)(2,1)S(1)}, bf16[1,128,1024]{2,1,0:T(8,128)(2,1)S(1)}, u32[]{:S(2)}, u32[]{:S(2)}) %collective-permute-start.7) | collective-permute-done | bytes 262176 | tf_op jit(solution)/shard_map/ppermute | solution.py:42
  112.8 2.0 %collective-permute-done.6.refs_4_ = bf16[1,128,1024]{2,1,0:T(8,128)(2,1)S(1)} collective-permute-done((bf16[1,128,1024]{2,1,0:T(8,128)(2,1)S(1)}, bf16[1,128,1024]{2,1,0:T(8,128)(2,1)S(1)}, u32[]{:S(2)}, u32[]{:S(2)}) %collective-permute-start.6) | collective-permute-done | bytes 262176 | tf_op jit(solution)/shard_map/ppermute | solution.py:42
  114.8 0.7 copy-done.6
  115.5 0.0 collective-permute-done.9.refs_7_
  115.5 0.0 copy-done.1
  115.6 8.2 %ladder_matmul.1 = bf16[8,128,2048]{2,1,0:T(8,128)(2,1)} custom-call(s32[1]{0:T(128)} %bitcast.pos.refs_0_, bf16[2,128,1024]{2,1,0:T(8,128)(2,1)} %bitcast.7, bf16[2,128,1024]{2,1,0:T(8,128)(2,1)} %copy-done.3, bf16[2,128,1024]{2,1,0:T(8,128)(2,1)} %copy-done.2, bf16[1,128,1024]{2,1,0:T(8,128)(2,1)} %copy-done.6, bf16[1,128,1024]{2,1,0:T(8,128)(2,1)} %copy-done.5, ...), custom_call_target="tpu_custom_call" | custom-call | tf_op jit(solution)/shard_map/ladder_matmul/pallas_call | solution.py:124
  (11 shorter events, 0.1 us)
Async XLA Ops:
  1.8 19.7 %collective-permute-start.8 = (bf16[64,2048]{1,0:T(8,128)(2,1)}, bf16[64,2048]{1,0:T(8,128)(2,1)S(1)}, u32[]{:S(2)}, u32[]{:S(2)}) collective-permute-start(bf16[64,2048]{1,0:T(8,128)(2,1)} %get-tuple-element.8), channel_id=1, source_target_pairs={{0,64},{64,0},{1,65},{65,1},{2,66},{66,2},{3,67},{67,3},{4,68},{68... | collective-permute-start | bytes 786440 | tf_op jit(solution)/shard_map/ppermute | solution.py:46
  22.7 30.3 %copy-start.4 = (bf16[32,1024]{1,0:T(8,128)(2,1)S(1)}, bf16[32,1024]{1,0:T(8,128)(2,1)}, u32[]{:S(2)}) copy-start(bf16[32,1024]{1,0:T(8,128)(2,1)} %get-tuple-element.7) | copy-start | bytes 196612
  51.1 64.5 %copy-start = (bf16[4,128,2048]{2,1,0:T(8,128)(2,1)}, bf16[4,128,2048]{2,1,0:T(8,128)(2,1)S(1)}, u32[]{:S(2)}) copy-start(bf16[4,128,2048]{2,1,0:T(8,128)(2,1)S(1)} %all_to_all.5.refs_6_) | copy-start | bytes 6291460
  51.1 64.5 %collective-permute-start.9 = (bf16[4,128,2048]{2,1,0:T(8,128)(2,1)S(1)}, bf16[4,128,2048]{2,1,0:T(8,128)(2,1)}, u32[]{:S(2)}, u32[]{:S(2)}) collective-permute-start(bf16[4,128,2048]{2,1,0:T(8,128)(2,1)S(1)} %all_to_all.5.refs_6_), channel_id=1, source_target_pairs={{0,32},{32,0},{1,33},{33,1},{2,34},{34,2},{3,35},{35,3},{4,36},{36... | collective-permute-start | bytes 6291464 | tf_op jit(solution)/shard_map/ppermute | solution.py:46
  53.0 11.3 %collective-permute-start = (bf16[32,1024]{1,0:T(8,128)(2,1)S(1)}, bf16[32,1024]{1,0:T(8,128)(2,1)S(1)}, u32[]{:S(2)}, u32[]{:S(2)}) collective-permute-start(bf16[32,1024]{1,0:T(8,128)(2,1)S(1)} %copy-done.4), channel_id=1, source_target_pairs={{0,16},{4,20},{8,24},{12,28},{16,0},{20,4},{24,8},{28,12},{1,17},{... | collective-permute-start | bytes 196616 | tf_op jit(solution)/shard_map/ppermute | solution.py:42
  64.3 10.7 %collective-permute-start.3 = (bf16[2,1,32,1024]{3,2,1,0:T(8,128)(2,1)S(1)}, bf16[2,1,32,1024]{3,2,1,0:T(8,128)(2,1)S(1)}, u32[]{:S(2)}, u32[]{:S(2)}) collective-permute-start(bf16[2,1,32,1024]{3,2,1,0:T(8,128)(2,1)S(1)} %pad_maximum_fusion.2), channel_id=1, source_target_pairs={{0,3},{1,2},{2,1},{3,0},{4,7},{5,6},{6,5},{7,4},{8,11},{9,10},{10,... | collective-permute-start | bytes 393224 | tf_op jit(solution)/shard_map/ppermute | solution.py:50
  70.6 11.9 %collective-permute-start.2 = (bf16[2,1,32,1024]{3,2,1,0:T(8,128)(2,1)S(1)}, bf16[2,1,32,1024]{3,2,1,0:T(8,128)(2,1)S(1)}, u32[]{:S(2)}, u32[]{:S(2)}) collective-permute-start(bf16[2,1,32,1024]{3,2,1,0:T(8,128)(2,1)S(1)} %pad_maximum_fusion.2), channel_id=1, source_target_pairs={{0,2},{1,3},{2,0},{3,1},{4,6},{5,7},{6,4},{7,5},{8,10},{9,11},{10,... | collective-permute-start | bytes 393224 | tf_op jit(solution)/shard_map/ppermute | solution.py:50
  72.6 10.0 %collective-permute-start.1 = (bf16[2,1,32,1024]{3,2,1,0:T(8,128)(2,1)S(1)}, bf16[2,1,32,1024]{3,2,1,0:T(8,128)(2,1)S(1)}, u32[]{:S(2)}, u32[]{:S(2)}) collective-permute-start(bf16[2,1,32,1024]{3,2,1,0:T(8,128)(2,1)S(1)} %pad_maximum_fusion.2), channel_id=1, source_target_pairs={{0,1},{1,0},{2,3},{3,2},{4,5},{5,4},{6,7},{7,6},{8,9},{9,8},{10,11... | collective-permute-start | bytes 393224 | tf_op jit(solution)/shard_map/ppermute | solution.py:50
  82.6 32.9 %copy-start.1 = (bf16[2,4,32,1024]{3,2,1,0:T(8,128)(2,1)}, bf16[2,4,32,1024]{3,2,1,0:T(8,128)(2,1)S(1)}, u32[]{:S(2)}) copy-start(bf16[2,4,32,1024]{3,2,1,0:T(8,128)(2,1)S(1)} %pad_maximum_fusion) | copy-start | bytes 1572868
  82.6 19.4 %collective-permute-start.5 = (bf16[2,128,1024]{2,1,0:T(8,128)(2,1)S(1)}, bf16[2,128,1024]{2,1,0:T(8,128)(2,1)S(1)}, u32[]{:S(2)}, u32[]{:S(2)}) collective-permute-start(bf16[2,128,1024]{2,1,0:T(8,128)(2,1)S(1)} %bitcast.5), channel_id=1, source_target_pairs={{0,4},{4,8},{8,12},{12,16},{16,20},{20,24},{24,28},{28,0},{1,5},{5... | collective-permute-start | bytes 1572872 | tf_op jit(solution)/shard_map/ppermute | solution.py:42
  86.0 18.0 %collective-permute-start.4 = (bf16[2,128,1024]{2,1,0:T(8,128)(2,1)S(1)}, bf16[2,128,1024]{2,1,0:T(8,128)(2,1)S(1)}, u32[]{:S(2)}, u32[]{:S(2)}) collective-permute-start(bf16[2,128,1024]{2,1,0:T(8,128)(2,1)S(1)} %bitcast.6), channel_id=1, source_target_pairs={{0,28},{4,0},{8,4},{12,8},{16,12},{20,16},{24,20},{28,24},{1,29},{... | collective-permute-start | bytes 1572872 | tf_op jit(solution)/shard_map/ppermute | solution.py:42
  102.0 13.5 %copy-start.2 = (bf16[2,128,1024]{2,1,0:T(8,128)(2,1)}, bf16[2,128,1024]{2,1,0:T(8,128)(2,1)S(1)}, u32[]{:S(2)}) copy-start(bf16[2,128,1024]{2,1,0:T(8,128)(2,1)S(1)} %collective-permute-done.5.refs_3_) | copy-start | bytes 1572868
  102.0 10.8 %collective-permute-start.7 = (bf16[1,128,1024]{2,1,0:T(8,128)(2,1)S(1)}, bf16[1,128,1024]{2,1,0:T(8,128)(2,1)S(1)}, u32[]{:S(2)}, u32[]{:S(2)}) collective-permute-start(bf16[1,128,1024]{2,1,0:T(8,128)(2,1)S(1)} %slice.9), channel_id=1, source_target_pairs={{0,4},{4,8},{8,12},{12,16},{16,20},{20,24},{24,28},{28,0},{1,5},{5... | collective-permute-start | bytes 786440 | tf_op jit(solution)/shard_map/ppermute | solution.py:42
  104.0 0.8 copy-start.3
  104.8 10.0 %collective-permute-start.6 = (bf16[1,128,1024]{2,1,0:T(8,128)(2,1)S(1)}, bf16[1,128,1024]{2,1,0:T(8,128)(2,1)S(1)}, u32[]{:S(2)}, u32[]{:S(2)}) collective-permute-start(bf16[1,128,1024]{2,1,0:T(8,128)(2,1)S(1)} %slice.8), channel_id=1, source_target_pairs={{0,28},{4,0},{8,4},{12,8},{16,12},{20,16},{24,20},{28,24},{1,29},{... | collective-permute-start | bytes 786440 | tf_op jit(solution)/shard_map/ppermute | solution.py:42
  112.8 2.8 %copy-start.5 = (bf16[1,128,1024]{2,1,0:T(8,128)(2,1)}, bf16[1,128,1024]{2,1,0:T(8,128)(2,1)S(1)}, u32[]{:S(2)}) copy-start(bf16[1,128,1024]{2,1,0:T(8,128)(2,1)S(1)} %collective-permute-done.7.refs_5_) | copy-start | bytes 786436
  114.8 0.7 copy-start.6
